TPU v7x, 256 devices: a whole 4x4x8 slice. The times are simulated.
256 devices in a mesh: chan: 128 (over z, y, x_lo, core), stn: 2 (over x_hi).
Axes of the slice: x: 4 (x_hi: 2, x_lo: 2; x = x_hi * 2 + x_lo), y: 4, z: 8, core: 2. Of those that a mesh axis runs over, the one named last changes fastest.
Arguments:
- voltages: bfloat16 [2, 1536, 2, 256, 512], P(None, 'chan', None, None, 'stn'), may hold values from -6 to 6
- delay_table: float32 [4096], replicated, may hold values from -8 to 8
- delay_index: int32 [64, 512], P(None, 'stn'), may hold values from 0 to 4094
- delay_fraction: int32 [64, 512], P(None, 'stn'), may hold values from 0 to 65535
- station_subarray: int32 [512], P('stn'), may hold values from 0 to 3
Outputs:
- beams: bfloat16 [2, 64, 2, 256, 1536], P(None, 'stn', None, 'chan')
All inputs are finite; a program needn't handle non-finite values.
Results may differ from a plain program's by a relative error of at most 0.0068.
Values may be sent and summed in bfloat16 or wider, within the bound.
A program may use at most 128 MiB of HBM per device.

v0:
```python
import math

import jax
import jax.numpy as jnp
from jax import lax
from jax.sharding import Mesh
from jax.sharding import PartitionSpec as P

STATIONS = 512
POL = 2
NFFT = 256
TAPS = 12
GROUPS = 4
CHAN = ("chan_0", "chan_1", "chan_2", "chan_3")


def joined_along(parts, dim):
    shape = list(parts.shape[1:])
    shape[dim] *= parts.shape[0]
    return jnp.moveaxis(parts, 0, dim).reshape(shape)


def all_blocks(x, axes, turns):
    parts = x[None]
    for k in turns:
        parts = lax.all_gather(parts, axes[k], axis=0, tiled=True)
    held = [lax.axis_size(axes[k]) for k in reversed(turns)]
    parts = parts.reshape(*held, *x.shape)
    turned = sorted(range(len(turns)), key=lambda place: turns[len(turns) - 1 - place])
    return parts.transpose(*turned, *range(len(turns), parts.ndim)).reshape(-1, *x.shape)


def gather_axes(x, axes, turns, dim):
    return joined_along(all_blocks(x, axes, turns), dim)


def passed_along(value, axis, steps):
    count = lax.axis_size(axis)
    initial, last = (max(0, -steps), min(count, count - steps))
    return lax.ppermute(value, axis, [(source, source + steps) for source in range(initial, last)])


def in_blocks(x, dim, peers):
    shape = x.shape
    parts = x.reshape(*shape[:dim], peers, shape[dim] // peers, *shape[dim + 1 :])
    return jnp.moveaxis(parts, dim, 0)


def sent_and_summed(x, axis, dim):
    parts = in_blocks(x, dim, lax.axis_size(axis))
    arrived = lax.all_to_all(parts, axis, split_axis=0, concat_axis=0, tiled=True)
    return arrived.sum(axis=0)


def prototype(tap_count, points):
    length = tap_count * points
    sample_ids = jnp.arange(length, dtype=jnp.float32)
    centred = (sample_ids - (length - 1) / 2.0) / points
    window = 0.5 - 0.5 * jnp.cos(2.0 * math.pi * (sample_ids + 0.5) / length)
    coeffs = jnp.sinc(centred) * window
    coeffs = coeffs * jnp.sqrt(points / jnp.sum(coeffs * coeffs))
    return coeffs.reshape(tap_count, points)


def dft_table(points):
    indices = jnp.arange(points, dtype=jnp.int32)
    product = indices[:, None] * indices[None, :] % points
    angles = 2.0 * math.pi / points * product.astype(jnp.float32)
    cosine = jnp.cos(angles) / math.sqrt(points)
    sine_part = jnp.sin(angles) / math.sqrt(points)
    real_input = jnp.stack([cosine, -sine_part], axis=1)
    imag_input = jnp.stack([sine_part, cosine], axis=1)
    return jnp.stack([real_input, imag_input], axis=0).astype(jnp.bfloat16)


def polyphase(padded, coeffs, frame_count):
    summed = jnp.zeros(padded.shape[:1] + (frame_count,) + padded.shape[2:], jnp.float32)
    for tap_index in range(coeffs.shape[0]):
        summed = summed + coeffs[tap_index][:, None] * padded[
            :, tap_index : tap_index + frame_count
        ].astype(jnp.float32)
    return summed.astype(jnp.bfloat16)


def steering(delays, station_subarray, channel_ids):
    beam_ids = jnp.arange(delays.shape[0], dtype=jnp.int32)
    member = (station_subarray[None, :] == (beam_ids % GROUPS)[:, None]).astype(
        jnp.float32
    ) * math.sqrt(GROUPS / STATIONS)
    signed = (channel_ids + NFFT // 2) % NFFT - NFFT // 2
    frequency = signed.astype(jnp.float32) / NFFT
    phases = -2.0 * math.pi * frequency[:, None, None] * delays[None, :, :]
    real_weight = (member * jnp.cos(phases)).astype(jnp.bfloat16)
    imag_weight = (member * jnp.sin(phases)).astype(jnp.bfloat16)
    first_row = jnp.stack([real_weight, -imag_weight], axis=2)
    second_row = jnp.stack([imag_weight, real_weight], axis=2)
    return jnp.stack([first_row, second_row], axis=1)


def shards(voltages, delay_table, delay_index, delay_fraction, station_subarray):
    frames_dev = voltages.shape[1]
    local_stations = voltages.shape[4]
    beam_count = delay_index.shape[0]
    groups_chan = lax.axis_size(CHAN)
    per_dev = NFFT // groups_chan
    share = beam_count * local_stations // groups_chan
    first_entry = lax.axis_index(CHAN) * share
    index_share = lax.dynamic_slice_in_dim(delay_index.reshape(-1), first_entry, share, 0)
    fraction_share = lax.dynamic_slice_in_dim(delay_fraction.reshape(-1), first_entry, share, 0)
    lower_delay = jnp.take(delay_table, index_share, axis=0)
    upper_delay = jnp.take(delay_table, index_share + 1, axis=0)
    delay_share = lower_delay + fraction_share.astype(jnp.float32) * (1.0 / 65536.0) * (
        upper_delay - lower_delay
    )
    delays = gather_axes(delay_share, CHAN, (2, 0, 1, 3), 0).reshape(beam_count, local_stations)
    coeffs = prototype(TAPS, NFFT)
    history = passed_along(voltages[:, frames_dev - (TAPS - 1) :], CHAN, 1)
    filtered = polyphase(jnp.concatenate([history, voltages], axis=1), coeffs, frames_dev)
    dft_full = dft_table(NFFT)
    spectra = lax.dot_general(
        dft_full, filtered, (((0, 1), (2, 3)), ((), ())), preferred_element_type=jnp.float32
    ).astype(jnp.bfloat16)
    channel_ids = lax.axis_index(CHAN) * per_dev + jnp.arange(per_dev, dtype=jnp.int32)
    weights = steering(delays, station_subarray, channel_ids)
    spectra = spectra.reshape(2, groups_chan, per_dev, POL, frames_dev, local_stations)
    partial_value = lax.dot_general(
        weights,
        lax.all_to_all(spectra, CHAN, split_axis=1, concat_axis=1, tiled=True),
        (((3, 4), (0, 5)), ((0,), (2,))),
        preferred_element_type=jnp.float32,
    )
    summed = sent_and_summed(partial_value, "stn", 2).astype(jnp.bfloat16)
    ordered = jnp.transpose(summed, (1, 2, 4, 0, 3, 5))
    return ordered.reshape(2, summed.shape[2], POL, per_dev, groups_chan * frames_dev)


def solution(mesh):
    torus = Mesh(
        mesh.devices.reshape(8, 4, 2, 2, mesh.shape["stn"]),
        ("chan_0", "chan_1", "chan_2", "chan_3", "stn"),
    )
    placed = (P(None, CHAN, None, None, "stn"), P(), P(None, "stn"), P(None, "stn"), P("stn"))
    return jax.shard_map(
        shards,
        mesh=torus,
        in_specs=placed,
        out_specs=P(None, "stn", None, CHAN, None),
        check_vma=False,
    )
```

profile of v0, /device:TPU:24, one launch (start us, length us, event | category | flops | bytes accessed | tf_op | source)
XLA Modules:
  0.0 368.2 jit_solution(15485896743960134796)
XLA Ops:
  0.0 0.0 copy-start
  0.0 0.0 slice-start
  0.0 5.9 %slice.85 = bf16[2,11,2,256,256]{4,3,2,1,0:T(8,128)(2,1)} slice(bf16[2,12,2,256,256]{4,3,2,1,0:T(8,128)(2,1)} %param.7), slice={[0:2], [1:12], [0:2], [0:256], [0:256]} | slice | bytes 11534336 | tf_op jit(solution)/shard_map/slice | solution.py:117
  5.9 1.9 collective-permute-start
  7.8 0.7 multiply_reduce_fusion
  9.2 0.1 broadcast_multiply_fusion
  9.3 1.0 fusion.16
  10.3 1.1 negate_convert_fusion
  11.4 0.0 slice-start.1
  11.5 62.3 %collective-permute-done = bf16[2,11,2,256,256]{4,3,2,1,0:T(8,128)(2,1)} collective-permute-done((bf16[2,11,2,256,256]{4,3,2,1,0:T(8,128)(2,1)}, bf16[2,11,2,256,256]{4,3,2,1,0:T(8,128)(2,1)}, u32[]{:S(2)}, u32[]{:S(2)}) %collective-permute-start) | collective-permute-done | bytes 5767200 | tf_op jit(solution)/shard_map/ppermute | solution.py:40
  73.8 5.8 %constant_dynamic-update-slice_fusion.1 = bf16[2,23,2,256,256]{4,3,2,1,0:T(8,128)(2,1)} fusion(bf16[2,11,2,256,256]{4,3,2,1,0:T(8,128)(2,1)} %collective-permute-done), kind=kLoop, calls=%fused_computation.83 | loop fusion | bytes 11534336
  79.6 0.0 slice-done
  79.6 0.0 slice-done.1
  79.6 3.1 constant_dynamic-update-slice_fusion
  82.7 31.7 %bitcast_convert_fusion = bf16[2,256,2,12,256]{4,1,3,2,0:T(8,128)(2,1)} fusion(bf16[2,12,2,256,256]{4,3,2,1,0:T(8,128)(2,1)S(1)} %bitcast.60, f32[256]{0:T(256)S(1)} %get-tuple-element.15, bf16[2,23,2,256,256]{4,3,2,1,0:T(8,128)(2,1)} %constant_dynamic-update-slice_fusion, f32[256]{0:T(256)S(1)} %get-tuple-element.16, f32[256]{0:T(256)S(1)} %get-tuple-element.17, ...), kind=kOutput, calls=%fused_computation.2 | convolution fusion | flops 3338665984 | bytes 82325504 | tf_op jit(solution)/shard_map/dot_general | solution.py:120
  114.4 0.0 copy-start.1
  114.4 0.0 copy-start.2
  114.4 0.0 copy-start.3
  114.4 12.8 %copy.29 = bf16[2,256,2,12,256]{4,0,3,2,1:T(2,128)(2,1)} copy(bf16[2,256,2,12,256]{4,1,3,2,0:T(8,128)(2,1)} %bitcast_convert_fusion) | data formatting | bytes 12582912 | tf_op jit(solution)/shard_map/reshape | solution.py:125
  127.2 13.8 %all-to-all-start = ((bf16[2,128,2,2,12,256]{5,0,4,3,2,1:T(2,128)(2,1)}), bf16[2,128,2,2,12,256]{5,0,4,3,2,1:T(2,128)(2,1)}, u32[]{:S(2)}, u32[]{:S(2)}) async-start(bf16[2,128,2,2,12,256]{5,0,4,3,2,1:T(2,128)(2,1)} %bitcast.58), calls=%async_computation | async-start | bytes 12582912 | tf_op jit(solution)/shard_map/all_to_all | solution.py:128
  140.9 0.0 copy-done.1
  141.0 0.0 copy-done.2
  141.1 0.1 compare_select_fusion.2
  141.2 0.0 copy-done
  141.2 1.1 gather_fusion.1
  142.3 1.1 gather_fusion
  143.5 0.1 add_bitcast_fusion
  143.6 13.1 %all-gather.1 = f32[2,1,128]{2,1,0:T(1,128)S(1)} all-gather(f32[1,1,128]{2,1,0:T(1,128)S(1)} %add_bitcast_fusion), channel_id=2, replica_groups=mesh['chan_0'=8,'chan_1'=4,'chan_2'=2,'chan_3'=2,'stn'=2] {'chan_2'}, dimensions={0}, use_global_device_ids=true | all-gather | bytes 1536 | tf_op jit(solution)/shard_map/all_gather | solution.py:26
  156.7 131.0 %all-gather.2 = f32[8,2,128]{2,1,0:T(2,128)S(1)} all-gather(f32[1,2,128]{2,1,0:T(2,128)S(1)} %bitcast.75), channel_id=1, replica_groups=mesh['chan_0'=8,'chan_1'=4,'chan_2'=2,'chan_3'=2,'stn'=2] {'chan_0'}, dimensions={0}, use_global_device_ids=true | all-gather | bytes 9216 | tf_op jit(solution)/shard_map/all_gather | solution.py:26
  287.7 11.9 %all_gather.14 = f32[64,128]{1,0:T(8,128)S(1)} all-gather(f32[16,128]{1,0:T(8,128)S(1)} %bitcast.74), channel_id=1, replica_groups=mesh['chan_0'=8,'chan_1'=4,'chan_2'=2,'chan_3'=2,'stn'=2] {'chan_1'}, dimensions={0}, use_global_device_ids=true | all-gather | bytes 40960 | tf_op jit(solution)/shard_map/all_gather | solution.py:26
  299.6 1.8 all_gather.15
  301.4 0.1 copy.15
  301.5 0.0 copy-done.3
  301.6 0.1 compare_select_fusion
  301.6 0.5 fusion.18
  302.1 0.5 fusion.57
  302.7 0.0 all-to-all-done
  302.7 10.0 %fusion = f32[2,2,64,128,2,12,1]{3,2,6,5,4,1,0:T(8,128)S(1)} fusion(bf16[2,128,2,2,12,256,1]{5,0,4,3,2,1,6:T(2,128)(2,1)} %bitcast.19, bf16[2,1,64,2,256]{4,2,3,1,0:T(8,128)(2,1)S(1)} %get-tuple-element.11, bf16[2,1,64,2,256]{4,2,3,1,0:T(8,128)(2,1)S(1)} %get-tuple-element.10), kind=kOutput, calls=%fused_computation.4 | convolution fusion | flops 805830656 | bytes 9699328 | tf_op jit(solution)/shard_map/dot_general | solution.py:126
  312.7 0.4 copy.40
  313.1 42.0 %all_to_all.10 = f32[2,2,2,32,128,2,12]{4,3,6,5,2,1,0:T(8,128)S(1)} all-to-all(f32[2,2,2,32,128,2,12]{4,3,6,5,2,1,0:T(8,128)S(1)} %bitcast.61), channel_id=1, replica_groups=mesh['chan_0'=8,'chan_1'=4,'chan_2'=2,'chan_3'=2,'stn'=2] {'stn'}, dimensions={0} | all-to-all | bytes 6291456 | tf_op jit(solution)/shard_map/all_to_all | solution.py:51
  355.1 1.4 reduce_sum.19
  356.5 6.6 %copy.22 = bf16[2,32,2,2,128,12]{1,3,5,4,2,0:T(2,128)(2,1)S(1)} copy(bf16[2,32,2,2,128,12]{4,1,5,2,0,3:T(8,128)(2,1)} %bitcast.64) | data formatting | bytes 1572864 | tf_op jit(solution)/shard_map/convert_element_type | solution.py:132
  363.2 5.0 %copy.23 = bf16[2,32,2,2,1536]{4,3,2,1,0:T(2,128)(2,1)} copy(bf16[2,32,2,2,1536]{1,3,4,2,0:T(2,128)(2,1)S(1)} %bitcast.63) | data formatting | bytes 1572864 | tf_op jit(solution)/shard_map/reshape | solution.py:134
  (10 shorter events, 0.2 us)
Async XLA Ops:
  0.0 141.2 %copy-start = (f32[4096]{0:T(1024)S(1)}, f32[4096]{0:T(1024)}, u32[]{:S(2)}) copy-start(f32[4096]{0:T(1024)} %param.8) | copy-start | bytes 49156
  0.0 79.6 %slice-start = ((s8[6291456]{0:T(1024)(128)(4,1)}), s8[2097152]{0:T(1024)(128)(4,1)S(1)}, s32[]{:S(2)}) async-start(s8[6291456]{0:T(1024)(128)(4,1)} %bitcast.59), calls=%async_computation.2 | async-start | bytes 4194304
  5.9 67.9 %collective-permute-start = (bf16[2,11,2,256,256]{4,3,2,1,0:T(8,128)(2,1)}, bf16[2,11,2,256,256]{4,3,2,1,0:T(8,128)(2,1)}, u32[]{:S(2)}, u32[]{:S(2)}) collective-permute-start(bf16[2,11,2,256,256]{4,3,2,1,0:T(8,128)(2,1)} %slice.85), channel_id=1, source_target_pairs={{0,2},{2,4},{4,6},{6,8},{8,10},{10,12},{12,14},{14,16},{16,18},{18... | collective-permute-start | bytes 17301512 | tf_op jit(solution)/shard_map/ppermute | solution.py:40
  11.4 68.1 %slice-start.1 = ((s8[6291456]{0:T(1024)(128)(4,1)}), s8[4194304]{0:T(1024)(128)(4,1)S(1)}, s32[]{:S(2)}) async-start(s8[6291456]{0:T(1024)(128)(4,1)} %bitcast.59), calls=%async_computation.3 | async-start | bytes 8388608
  114.4 26.6 %copy-start.1 = (s32[64,256]{1,0:T(8,128)S(1)}, s32[64,256]{1,0:T(8,128)}, u32[]{:S(2)}) copy-start(s32[64,256]{1,0:T(8,128)} %param.10) | copy-start | bytes 196612
  114.4 26.6 %copy-start.2 = (s32[64,256]{1,0:T(8,128)S(1)}, s32[64,256]{1,0:T(8,128)}, u32[]{:S(2)}) copy-start(s32[64,256]{1,0:T(8,128)} %param.9) | copy-start | bytes 196612
  114.4 187.2 %copy-start.3 = (s32[256]{0:T(256)S(1)}, s32[256]{0:T(256)}, u32[]{:S(2)}) copy-start(s32[256]{0:T(256)} %param.11) | copy-start | bytes 3076
  127.2 175.5 %all-to-all-start = ((bf16[2,128,2,2,12,256]{5,0,4,3,2,1:T(2,128)(2,1)}), bf16[2,128,2,2,12,256]{5,0,4,3,2,1:T(2,128)(2,1)}, u32[]{:S(2)}, u32[]{:S(2)}) async-start(bf16[2,128,2,2,12,256]{5,0,4,3,2,1:T(2,128)(2,1)} %bitcast.58), calls=%async_computation | async-start | bytes 12582912 | tf_op jit(solution)/shard_map/all_to_all | solution.py:128
where the time goes:
time: 369 us; the launch traced here: 368 us
  blocking collectives  200 us (54%)
  waiting for transfers between devices  62.3 us (17%)
  local copies, waits for them, and re-layouts  42.1 us (11%)
  matrix products  41.7 us (11%)
  starting transfers between devices  15.7 us (4%)
  other arithmetic  5.62 us (2%)
    all_gather x4, blocking collectives, all_blocks(): parts = lax.all_gather(parts, axes[k], axis=0, tiled=True)  158 us
    ppermute x1, waiting for transfers between devices, passed_along(): lax.ppermute(value, axis, [(source, source + steps) for source in range(i...  62.3 us
    all_to_all x1, blocking collectives, sent_and_summed(): lax.all_to_all(parts, axis, split_axis=0, concat_axis=0, tiled=True)  42 us
    dot_general x1, matrix products, shards(): lax.dot_general(dft_full, filtered, (((0, 1), (2, 3)), ((), ())), preferr...  31.7 us
    all_to_all x1, starting transfers between devices, shards(): lax.all_to_all(spectra, CHAN, split_axis=1, concat_axis=1, tiled=True)  13.8 us
    reshape x1, local copies, waits for them, and re-layouts, shards(): spectra.reshape(2, groups_chan, per_dev, POL, frames_dev, local_stations)  12.8 us
    dot_general x1, matrix products, shards(): lax.dot_general(weights, lax.all_to_all(spectra, CHAN, split_axis=1, conc...  10 us
  transfers between devices with their start and end apart: 2, of which 1 were waited for; matrix products, arithmetic and copies ran while one was open for 2% of the time, Pallas kernels for 0%

commit v1 on v0

v1 whole, which is shorter than its diff:
```python
import functools
import math

import jax
import jax.numpy as jnp
import numpy as np
from jax import lax
from jax.experimental import pallas as pl
from jax.experimental.pallas import tpu as pltpu
from jax.sharding import Mesh
from jax.sharding import PartitionSpec as P

STATIONS = 512
POL = 2
NFFT = 256
TAPS = 12
GROUPS = 4
CHAN = ("z", "y", "xl", "core")
MESH = pl.DeviceIdType.MESH
F32 = jnp.float32
BF16 = jnp.bfloat16
OUT = 2 * TAPS
KB = 16


def prototype():
    length = TAPS * NFFT
    n = np.arange(length, dtype=np.float64)
    h = np.sinc((n - (length - 1) / 2.0) / NFFT) * (0.5 - 0.5 * np.cos(2.0 * np.pi * (n + 0.5) / length))
    h = h * np.sqrt(NFFT / np.sum(h * h))
    return h.reshape(TAPS, NFFT)


def filter_rows():
    coeffs = prototype()
    rows = np.zeros((2, NFFT // KB, OUT, TAPS, KB), np.float32)
    for out in range(OUT - 1):
        for frame in range(TAPS):
            tap = frame - out + TAPS - 1
            if 0 <= tap < TAPS:
                block = coeffs[tap].reshape(NFFT // KB, KB)
                rows[0, :, out, frame] = block
                rows[1, :, (out + TAPS) % OUT, frame] = block
    return rows.reshape(2, NFFT // KB, OUT, TAPS * KB)


def dft_rows():
    k = np.arange(NFFT)
    angle = (np.float32(2.0 * np.pi / NFFT) * (k[:, None] * k[None, :] % NFFT).astype(np.float32)).astype(np.float32)
    cosine = np.cos(angle).astype(np.float32) / np.float32(math.sqrt(NFFT))
    sine = np.sin(angle).astype(np.float32) / np.float32(math.sqrt(NFFT))
    half = NFFT // 2
    lower = sine[:half].copy()
    lower[0] = cosine[half]
    return np.concatenate([cosine[:half], lower], axis=0)


def beams_kernel(v_ref, rows_ref, dft_ref, table_ref, step_ref, index_ref, fraction_ref, group_ref, out_ref,
                 filt, spec, weight, lists):
    half = NFFT // 2
    stn = v_ref.shape[-1]
    beams = index_ref.shape[0]
    own = beams // GROUPS
    group = group_ref[...]
    index = jnp.zeros((own, stn), jnp.int32)
    fraction = jnp.zeros((own, stn), jnp.int32)
    parts = stn // 128
    for part in range(parts):
        lists[part] = index_ref[:, part * 128:(part + 1) * 128]
        lists[parts + part] = fraction_ref[:, part * 128:(part + 1) * 128]

    def every_fourth(start, g):
        return jnp.concatenate([lists[start + part, pl.ds(g, own, stride=GROUPS), :] for part in range(parts)], axis=1)

    for g in range(GROUPS):
        index = jnp.where(group == g, every_fourth(0, g), index)
        fraction = jnp.where(group == g, every_fourth(parts, g), fraction)
    upper, lower = index // 128, index % 128

    def look(row, found):
        base, rise = found
        here = upper == row
        b_row = jnp.broadcast_to(table_ref[pl.ds(row, 1), :], (own, 128))
        s_row = jnp.broadcast_to(step_ref[pl.ds(row, 1), :], (own, 128))
        b_new, s_new = [], []
        for part in range(stn // 128):
            at = lower[:, part * 128:(part + 1) * 128]
            b_new.append(jnp.take_along_axis(b_row, at, axis=1, mode="promise_in_bounds"))
            s_new.append(jnp.take_along_axis(s_row, at, axis=1, mode="promise_in_bounds"))
        return jnp.where(here, jnp.concatenate(b_new, 1), base), jnp.where(here, jnp.concatenate(s_new, 1), rise)

    zero = jnp.zeros((own, stn), F32)
    base, rise = lax.fori_loop(0, table_ref.shape[0], look, (zero, zero))
    delays = base + fraction.astype(F32) * (1.0 / 65536.0) * rise
    angle = delays * (-2.0 * math.pi / NFFT)
    turn_re, turn_im = jnp.cos(angle), jnp.sin(angle)
    masks = [jnp.where(group == g, math.sqrt(GROUPS / STATIONS), 0.0) for g in range(GROUPS)]

    lane = lax.broadcasted_iota(jnp.int32, (OUT, KB, TAPS * KB), 2) % KB
    row = lax.broadcasted_iota(jnp.int32, (OUT, KB, TAPS * KB), 1)
    diagonal = lane == row

    def filter_block(kb, _):
        lhs = jnp.where(diagonal, rows_ref[kb][:, None, :], 0.0).reshape(OUT * KB, TAPS * KB).astype(BF16)
        at = pl.ds(pl.multiple_of(kb * KB, KB), KB)
        for p in range(POL):
            for i in range(2):
                rhs = v_ref[p, :, i, at, :].reshape(TAPS * KB, stn)
                made = jnp.dot(lhs, rhs, preferred_element_type=F32)
                filt[p * OUT:(p + 1) * OUT, i, at, :] = made.reshape(OUT, KB, stn).astype(BF16)
        return 0

    lax.fori_loop(0, NFFT // KB, filter_block, 0)

    first = lax.broadcasted_iota(jnp.int32, (half, stn), 0) == 0

    def transform(frame, _):
        r = jnp.dot(dft_ref[...], filt[frame, 0], preferred_element_type=F32)
        m = jnp.dot(dft_ref[...], filt[frame, 1], preferred_element_type=F32)
        c_re, s_re, c_im, s_im = r[:half], r[half:], m[:half], m[half:]
        at = pl.ds(pl.multiple_of(frame * half, half), half)
        values = (
            jnp.where(first, c_re, c_re + s_im),
            jnp.where(first, c_im, c_im - s_re),
            jnp.where(first, s_re, c_re - s_im),
            jnp.where(first, s_im, c_im + s_re),
        )
        for which, value in enumerate(values):
            for part in range(stn // 128):
                spec[which, part, at, :] = value[:, part * 128:(part + 1) * 128]
        return 0

    lax.fori_loop(0, POL * OUT, transform, 0)

    rows = POL * OUT
    lanes = lax.broadcasted_iota(jnp.int32, (rows, 128), 1)
    minus_low = jnp.where(lanes < 64, -1.0, 1.0)
    minus_high = -minus_low
    even_chunk = lanes[:OUT] // 32 % 2 == 0
    top = lax.broadcasted_iota(jnp.int32, (OUT, 128), 0) < TAPS

    def take(which, c):
        parts = [spec[which, part, pl.ds(c, rows, stride=half), :] for part in range(stn // 128)]
        return jnp.concatenate(parts, axis=1).astype(BF16)

    def weights(w_re, w_im):
        parts = []
        for value in (w_re, w_im):
            for h in range(2):
                for g in range(GROUPS):
                    parts.append(value[h * own // 2:(h + 1) * own // 2] * masks[g])
        weight[...] = jnp.concatenate(parts, axis=0).astype(BF16)

    def times(lhs):
        return lax.dot_general(lhs, weight[...], (((1,), (1,)), ((), ())), preferred_element_type=F32)

    def positive(re, im):
        return re + minus_low * pltpu.roll(im, 64, 1)

    def negative(re, im):
        return minus_high * re + pltpu.roll(im, 64, 1)

    def both(c, w_re, w_im):
        weights(w_re, w_im)
        made = times(jnp.concatenate([take(which, c) for which in range(4)], axis=0))
        return (positive(made[:rows], made[rows:2 * rows]), negative(made[2 * rows:3 * rows], made[3 * rows:]))

    def by_half(value):
        a, b = value[:OUT], value[OUT:]
        return (jnp.where(even_chunk, a, pltpu.roll(b, 32, 1)), jnp.where(even_chunk, pltpu.roll(a, 96, 1), b))

    def put(owner, even, odd):
        zy, at = owner // 4, owner % 4
        xl, core = at // 2, at % 2
        for h, (e, o) in enumerate(zip(by_half(even), by_half(odd))):
            out_ref[core, h, xl, zy, 0] = jnp.where(top, e, pltpu.roll(o, TAPS, 0)).astype(BF16)
            out_ref[core, h, xl, zy, 1] = jnp.where(top, pltpu.roll(e, TAPS, 0), o).astype(BF16)

    def turned(w):
        return (w[0] * turn_re - w[1] * turn_im, w[0] * turn_im + w[1] * turn_re)

    w = (jnp.ones((own, stn), F32), zero)
    even, _ = both(0, *w)
    w = turned(w)
    odd, carried = both(1, *w)
    w = turned(w)
    put(0, even, odd)

    def pair(d, state):
        w_re, w_im, kept = state
        even, even_minus = both(2 * d, w_re, w_im)
        w = turned((w_re, w_im))
        odd, odd_minus = both(2 * d + 1, *w)
        w = turned(w)
        put(d, even, odd)
        put(half - d, even_minus, kept)
        return w[0], w[1], odd_minus

    w_re, w_im, carried = lax.fori_loop(1, half // 2, pair, (w[0], w[1], carried))
    weights(w_re, w_im)
    made = times(jnp.concatenate([take(2, 0), take(3, 0)], axis=0))
    put(half // 2, negative(made[:rows], made[rows:]), carried)


def beams_call(v, rows, dft, table, step, index, fraction, group, zy):
    stn = v.shape[-1]
    vmem = pl.BlockSpec(memory_space=pltpu.VMEM)
    return pl.pallas_call(
        beams_kernel,
        out_shape=jax.ShapeDtypeStruct((2, 2, 2, zy, 2, OUT, 128), BF16),
        in_specs=[vmem] * 8,
        out_specs=vmem,
        scratch_shapes=[
            pltpu.VMEM((POL * OUT, 2, NFFT, stn), BF16),
            pltpu.VMEM((4, stn // 128, POL * OUT * NFFT // 2, 128), F32),
            pltpu.VMEM((128, stn), BF16),
            pltpu.VMEM((stn // 64, index.shape[0], 128), jnp.int32),
        ],
        compiler_params=pltpu.CompilerParams(vmem_limit_bytes=60 * 1024 * 1024),
        name="partial_beams",
    )(v, rows, dft, table, step, index, fraction, group)


def exchange_kernel(nz, ny, pa, out, r0, m, r1, s2, s_sem, r_sem, local_sem, s1_sem, r1_sem, s2_sem, r2_sem):
    z, y = lax.axis_index("z"), lax.axis_index("y")
    xl, core, xh = lax.axis_index("xl"), lax.axis_index("core"), lax.axis_index("stn")
    zy = z * ny + y
    count = nz * ny

    def row_peer(k):
        place = (xh * 2 + xl + k) % 4
        return (z, y, place % 2, core, place // 2), place

    def column_peer(k):
        place = (zy + k) % count
        return (place // ny, place % ny, xl, core, xh), place

    barrier = pltpu.get_barrier_semaphore()
    pl.semaphore_signal(barrier, inc=1, device_id=(z, y, xl, 1 - core, xh), device_id_type=MESH)
    for k in range(1, 4):
        pl.semaphore_signal(barrier, inc=1, device_id=row_peer(k)[0], device_id_type=MESH)

    def greet(k, _):
        pl.semaphore_signal(barrier, inc=1, device_id=column_peer(k)[0], device_id_type=MESH)
        return 0

    lax.fori_loop(1, count, greet, 0)
    pl.semaphore_wait(barrier, 4 + count - 1)

    first = pltpu.make_async_remote_copy(
        src_ref=pa.at[1 - core], dst_ref=r0, send_sem=s_sem, recv_sem=r_sem,
        device_id=(z, y, xl, 1 - core, xh), device_id_type=MESH)
    first.start()
    first.wait()
    lead = core == 0

    def merge(h, x):
        def body(i, _):
            a0, a1 = pa[core, h, x, i, 0].astype(F32), pa[core, h, x, i, 1].astype(F32)
            b0, b1 = r0[h, x, i, 0].astype(F32), r0[h, x, i, 1].astype(F32)
            m[h, x, i, 0] = jnp.where(lead, a0, b0).astype(BF16)
            m[h, x, i, 1] = (a1 + b1).astype(BF16)
            m[h, x, i, 2] = jnp.where(lead, b0, a0).astype(BF16)
            return 0
        lax.fori_loop(0, count, body, 0)

    here = xh * 2 + xl
    sends = []
    for k in (2, 1, 3, 0):
        device, place = row_peer(k)
        merge(place // 2, place % 2)
        if k == 0:
            copy = pltpu.make_async_copy(m.at[place // 2, place % 2], r1.at[here], local_sem)
        else:
            copy = pltpu.make_async_remote_copy(
                src_ref=m.at[place // 2, place % 2], dst_ref=r1.at[here], send_sem=s1_sem.at[k - 1],
                recv_sem=r1_sem.at[k - 1], device_id=device, device_id_type=MESH)
        copy.start()
        sends.append(copy)
    for copy in sends:
        copy.wait()

    def reduce(i, _):
        t = [[r1[xx, i, g].astype(F32) + r1[2 + xx, i, g].astype(F32) for g in range(3)] for xx in range(2)]
        s2[i, 0] = t[0][0].astype(BF16)
        s2[i, 1] = t[0][1].astype(BF16)
        s2[i, 2] = (t[0][2] + t[1][0]).astype(BF16)
        s2[i, 3] = t[1][1].astype(BF16)
        s2[i, 4] = t[1][2].astype(BF16)
        return 0

    lax.fori_loop(0, count, reduce, 0)

    mine = pltpu.make_async_copy(s2.at[zy], out.at[zy], local_sem)
    mine.start()

    def column(k):
        device, place = column_peer(k)
        return pltpu.make_async_remote_copy(
            src_ref=s2.at[place], dst_ref=out.at[zy], send_sem=s2_sem.at[k], recv_sem=r2_sem.at[k],
            device_id=device, device_id_type=MESH)

    def send(k, _):
        column(k).start()
        return 0

    def finish(k, _):
        column(k).wait()
        return 0

    lax.fori_loop(1, count, send, 0)
    mine.wait()
    lax.fori_loop(1, count, finish, 0)


def exchange_call(pa, nz, ny):
    zy = nz * ny
    vmem = pl.BlockSpec(memory_space=pltpu.VMEM)
    dma = pltpu.SemaphoreType.DMA
    return pl.pallas_call(
        functools.partial(exchange_kernel, nz, ny),
        out_shape=jax.ShapeDtypeStruct((zy, 5, OUT, 128), BF16),
        in_specs=[vmem],
        out_specs=vmem,
        scratch_shapes=[
            pltpu.VMEM((2, 2, zy, 2, OUT, 128), BF16),
            pltpu.VMEM((2, 2, zy, 3, OUT, 128), BF16),
            pltpu.VMEM((4, zy, 3, OUT, 128), BF16),
            pltpu.VMEM((zy, 5, OUT, 128), BF16),
            dma, dma, dma, dma((3,)), dma((3,)), dma((zy,)), dma((zy,)),
        ],
        compiler_params=pltpu.CompilerParams(
            collective_id=0, has_side_effects=True, vmem_limit_bytes=48 * 1024 * 1024),
        name="exchange",
    )(pa)


def finish_kernel(x_ref, out_ref, frames):
    blocks = x_ref.shape[0]
    top = lax.broadcasted_iota(jnp.int32, (OUT, 128), 0) < TAPS
    span = 4 * TAPS

    def gather(b, _):
        segs = [x_ref[b, g].astype(F32) for g in range(4)]
        before = x_ref[jnp.maximum(b - 1, 0), 4].astype(F32)
        segs[0] = segs[0] + jnp.where(b > 0, before, 0.0)
        for j in range(2):
            a, c = segs[2 * j], segs[2 * j + 1]
            at = pl.ds(pl.multiple_of(b * span + j * OUT, 8), OUT)
            frames[0, at, :] = jnp.where(top, a, pltpu.roll(c, TAPS, 0))
            frames[1, at, :] = jnp.where(top, pltpu.roll(a, TAPS, 0), c)
        return 0

    lax.fori_loop(0, blocks, gather, 0)

    def turn(t, _):
        at = pl.ds(pl.multiple_of(t * 128, 128), 128)
        a, c = frames[0, at, :].T, frames[1, at, :].T
        both = jnp.stack([a, c], axis=1).astype(BF16)
        for ro in range(2):
            for p in range(POL):
                for g in range(GROUPS):
                    for jj in range(8):
                        out_ref[ro, 4 * jj + g, p, :, at] = both[ro * 64 + p * 32 + g * 8 + jj]
        return 0

    lax.fori_loop(0, blocks * span // 128, turn, 0)


def finish_call(x):
    blocks = x.shape[0]
    total = blocks * 4 * TAPS
    vmem = pl.BlockSpec(memory_space=pltpu.VMEM)
    return pl.pallas_call(
        finish_kernel,
        out_shape=jax.ShapeDtypeStruct((2, 32, POL, 2, total), BF16),
        in_specs=[vmem],
        out_specs=vmem,
        scratch_shapes=[pltpu.VMEM((2, total, 128), F32)],
        compiler_params=pltpu.CompilerParams(vmem_limit_bytes=32 * 1024 * 1024),
        name="finish",
    )(x)


def shards(voltages, delay_table, delay_index, delay_fraction, station_subarray):
    nz, ny = lax.axis_size("z"), lax.axis_size("y")
    rows = lax.dynamic_index_in_dim(jnp.asarray(filter_rows()), lax.axis_index("core"), 0, keepdims=False)
    dft = jnp.asarray(dft_rows()).astype(BF16)
    step = jnp.concatenate([delay_table[1:], delay_table[-1:]]) - delay_table
    pa = beams_call(voltages, rows, dft, delay_table.reshape(-1, 128), step.reshape(-1, 128), delay_index,
                    delay_fraction, station_subarray.reshape(1, -1), nz * ny)
    return finish_call(exchange_call(pa, nz, ny))


def solution(mesh):
    torus = Mesh(mesh.devices.reshape(8, 4, 2, 2, mesh.shape["stn"]), CHAN + ("stn",))
    placed = (P(None, CHAN, None, None, "stn"), P(), P(None, "stn"), P(None, "stn"), P("stn"))
    return jax.shard_map(
        shards,
        mesh=torus,
        in_specs=placed,
        out_specs=P(None, "stn", None, CHAN, None),
        check_vma=False,
    )
```

time: 369 us -> 135 us (0.37)
  blocking collectives: 200 us -> 0 us
  Pallas kernels: 0 us -> 127 us
  waiting for transfers between devices: 62.3 us -> 0 us
  matrix products: 41.7 us -> 0 us
  local copies, waits for them, and re-layouts: 42.1 us -> 5.71 us
  starting transfers between devices: 15.7 us -> 0 us
    all_gather x4 -> x0, blocking collectives: 158 us -> none  [all_blocks(): parts = lax.all_gather(parts, axes[k], axis=0, tiled=True)]
    pallas_call x0 -> x3, Pallas kernels: none -> 127 us  [the longest x1 67.7 us: exchange_call(): pl.pallas_call(functools.partial(exchange_kernel, nz, ny), out_shape=jax....]
    ppermute x1 -> x0, waiting for transfers between devices: 62.3 us -> none  [passed_along(): lax.ppermute(value, axis, [(source, source + steps) for source in range(i...]
    all_to_all x1 -> x0, blocking collectives: 42 us -> none  [sent_and_summed(): lax.all_to_all(parts, axis, split_axis=0, concat_axis=0, tiled=True)]
    dot_general x2 -> x0, matrix products: 41.7 us -> none  [the longest x1 31.7 us: shards(): lax.dot_general(dft_full, filtered, (((0, 1), (2, 3)), ((), ())), preferr...]
    reshape x4 -> x0, local copies, waits for them, and re-layouts: 18.3 us -> none  [the longest x1 12.8 us: shards(): spectra.reshape(2, groups_chan, per_dev, POL, frames_dev, local_stations)]
    all_to_all x1 -> x0, starting transfers between devices: 13.8 us -> none  [shards(): lax.all_to_all(spectra, CHAN, split_axis=1, concat_axis=1, tiled=True)]
    convert_element_type x1 -> x0, local copies, waits for them, and re-layouts: 6.64 us -> none  [shards(): summed = sent_and_summed(partial_value, 'stn', 2).astype(jnp.bfloat16)]
  transfers between devices with their start and end apart: 2 -> 0, of which waited for: 1 -> 0; matrix products, arithmetic and copies ran while one was open for 2% -> 0% of each run, Pallas kernels for 0% -> 0%
where the time goes in v1:
time: 135 us; the launch traced here: 134 us
  Pallas kernels  127 us (94%)
  local copies, waits for them, and re-layouts  5.71 us (4%)
  other arithmetic  2.04 us (2%)
    pallas_call x1, Pallas kernels, exchange_call(): pl.pallas_call(functools.partial(exchange_kernel, nz, ny), out_shape=jax....  67.7 us
    pallas_call x1, Pallas kernels, beams_call(): pl.pallas_call(beams_kernel, out_shape=jax.ShapeDtypeStruct((2, 2, 2, zy,...  55.5 us
    pallas_call x1, Pallas kernels, finish_call(): pl.pallas_call(finish_kernel, out_shape=jax.ShapeDtypeStruct((2, 32, POL,...  3.43 us

profile of v1, /device:TPU:24, one launch (start us, length us, event | category | flops | bytes accessed | tf_op | source)
XLA Modules:
  0.0 134.5 jit_solution(2248848851969111007)
XLA Ops:
  0.0 1.3 slice.7
  1.3 0.8 slice.6
  2.1 2.0 %fusion.step_ref = f32[32,128]{1,0:T(8,128)} fusion(f32[4096]{0:T(1024)} %param.8, f32[1]{0:T(128)} %slice.7, f32[4095]{0:T(1024)S(1)} %slice.6), kind=kLoop, calls=%fused_computation.2 | loop fusion | flops 8192 | bytes 49152 | tf_op jit(solution)/shard_map/reshape | solution.py:390
  4.1 1.8 %dynamic-slice_bitcast_fusion.rows_ref = f32[16,24,192]{2,1,0:T(8,128)} fusion(f32[2,16,24,192]{3,2,1,0:T(8,128)} %constant.14.clone, s32[]{:T(128)S(6)} %select_n.4), kind=kLoop, calls=%fused_computation | loop fusion | bytes 589828 | tf_op jit(solution)/shard_map/jit(dynamic_index_in_dim)/squeeze | solution.py:387
  5.9 55.5 %partial_beams.1.pa = bf16[2,2,2,32,2,24,128]{6,5,4,3,2,1,0:T(8,128)(2,1)} custom-call(bf16[2,12,2,256,256]{4,3,2,1,0:T(8,128)(2,1)} %v_ref.1, f32[16,24,192]{2,1,0:T(8,128)} %dynamic-slice_bitcast_fusion.rows_ref, bf16[256,256]{1,0:T(8,128)(2,1)} %constant.17.dft_ref, f32[32,128]{1,0:T(8,128)} %bitcast.6, f32[32,128]{1,0:T(8,128)} %fusion.step_ref, ...), custom_call_target="tpu_custom_call" | custom-call | tf_op jit(solution)/shard_map/partial_beams/pallas_call | solution.py:208
  61.4 0.0 copy-start
  61.4 1.9 %copy-done = bf16[2,2,2,32,2,24,128]{6,5,4,3,2,1,0:T(8,128)(2,1)S(1)} copy-done((bf16[2,2,2,32,2,24,128]{6,5,4,3,2,1,0:T(8,128)(2,1)S(1)}, bf16[2,2,2,32,2,24,128]{6,5,4,3,2,1,0:T(8,128)(2,1)}, u32[]{:S(2)}) %copy-start) | copy-done | bytes 3145752
  63.3 67.7 %exchange.1.x_ref = bf16[32,5,24,128]{3,2,1,0:T(8,128)(2,1)S(1)} custom-call(bf16[2,2,2,32,2,24,128]{6,5,4,3,2,1,0:T(8,128)(2,1)S(1)} %copy-done), custom_call_target="tpu_custom_call" | custom-call | tf_op jit(solution)/shard_map/exchange/pallas_call | solution.py:320
  131.0 3.4 %finish.1 = bf16[2,32,2,2,1536]{4,3,2,1,0:T(2,128)(2,1)} custom-call(bf16[32,5,24,128]{3,2,1,0:T(8,128)(2,1)S(1)} %exchange.1.x_ref), custom_call_target="tpu_custom_call" | custom-call | tf_op jit(solution)/shard_map/finish/pallas_call | solution.py:374
Async XLA Ops:
  61.4 1.9 %copy-start = (bf16[2,2,2,32,2,24,128]{6,5,4,3,2,1,0:T(8,128)(2,1)S(1)}, bf16[2,2,2,32,2,24,128]{6,5,4,3,2,1,0:T(8,128)(2,1)}, u32[]{:S(2)}) copy-start(bf16[2,2,2,32,2,24,128]{6,5,4,3,2,1,0:T(8,128)(2,1)} %partial_beams.1.pa) | copy-start | bytes 9437188

commit v2 on v1

v2 whole, which is shorter than its diff:
```python
import functools
import math

import jax
import jax.numpy as jnp
import numpy as np
from jax import lax
from jax.experimental import pallas as pl
from jax.experimental.pallas import tpu as pltpu
from jax.sharding import Mesh
from jax.sharding import PartitionSpec as P

STATIONS = 512
POL = 2
NFFT = 256
TAPS = 12
GROUPS = 4
CHAN = ("z", "y", "xl", "core")
MESH = pl.DeviceIdType.MESH
F32 = jnp.float32
BF16 = jnp.bfloat16
OUT = 2 * TAPS
CHUNKS = 8
LAG = 3
UNROLL_T = 2
UNROLL_P = 1
KB = 16


def prototype():
    length = TAPS * NFFT
    n = np.arange(length, dtype=np.float64)
    h = np.sinc((n - (length - 1) / 2.0) / NFFT) * (0.5 - 0.5 * np.cos(2.0 * np.pi * (n + 0.5) / length))
    h = h * np.sqrt(NFFT / np.sum(h * h))
    return h.reshape(TAPS, NFFT)


def filter_rows():
    coeffs = prototype()
    rows = np.zeros((NFFT // KB, OUT, TAPS, KB), np.float32)
    for out in range(OUT - 1):
        for frame in range(TAPS):
            tap = frame - out + TAPS - 1
            if 0 <= tap < TAPS:
                rows[:, out, frame] = coeffs[tap].reshape(NFFT // KB, KB)
    return rows.reshape(NFFT // KB, OUT, TAPS * KB)


def dft_rows():
    k = np.arange(NFFT)
    angle = (np.float32(2.0 * np.pi / NFFT) * (k[:, None] * k[None, :] % NFFT).astype(np.float32)).astype(np.float32)
    cosine = np.cos(angle).astype(np.float32) / np.float32(math.sqrt(NFFT))
    sine = np.sin(angle).astype(np.float32) / np.float32(math.sqrt(NFFT))
    half = NFFT // 2
    lower = sine[:half].copy()
    lower[0] = cosine[half]
    return np.concatenate([cosine[:half], lower], axis=0)


def fused_kernel(nz, ny, v_hbm, rows_ref, dft_ref, table_ref, index_ref, fraction_ref, group_ref, out,
                 vbuf, filt, spec, lists, pa, r0, m, r1, s2, v_sem, s0_sem, r0_sem, own_sem, s1_sem, r1_sem, s2_sem,
                 r2_sem, mine_sem):
    half = NFFT // 2
    stn = v_hbm.shape[-1]
    parts = stn // 128
    beams = index_ref.shape[0]
    own = beams // GROUPS
    z, y = lax.axis_index("z"), lax.axis_index("y")
    xl, core, xh = lax.axis_index("xl"), lax.axis_index("core"), lax.axis_index("stn")
    zy = z * ny + y
    count = nz * ny
    steps = half // 2 // CHUNKS
    side = count // CHUNKS // 2

    def row_peer(k):
        place = (xh * 2 + xl + k) % 4
        return (z, y, place % 2, core, place // 2), place

    def column_peer(k):
        place = (zy + k) % count
        return (place // ny, place % ny, xl, core, xh)

    other = (z, y, xl, 1 - core, xh)
    barrier = pltpu.get_barrier_semaphore()
    pl.semaphore_signal(barrier, inc=1, device_id=other, device_id_type=MESH)
    for k in range(1, 4):
        pl.semaphore_signal(barrier, inc=1, device_id=row_peer(k)[0], device_id_type=MESH)

    def greet(k, _):
        pl.semaphore_signal(barrier, inc=1, device_id=column_peer(k), device_id_type=MESH)
        return 0

    lax.fori_loop(1, count, greet, 0)

    def fetch(kb, slot):
        at = pl.ds(pl.multiple_of(kb * KB, KB), KB)
        return pltpu.make_async_copy(v_hbm.at[:, :, :, at, :], vbuf.at[slot], v_sem.at[slot])

    fetch(0, 0).start()

    group = group_ref[...]
    index = jnp.zeros((own, stn), jnp.int32)
    fraction = jnp.zeros((own, stn), jnp.int32)
    for part in range(parts):
        lists[part] = index_ref[:, part * 128:(part + 1) * 128]
        lists[parts + part] = fraction_ref[:, part * 128:(part + 1) * 128]

    def every_fourth(start, g):
        return jnp.concatenate([lists[start + part, pl.ds(g, own, stride=GROUPS), :] for part in range(parts)], axis=1)

    for g in range(GROUPS):
        index = jnp.where(group == g, every_fourth(0, g), index)
        fraction = jnp.where(group == g, every_fourth(parts, g), fraction)
    upper, lower = index // 128, index % 128
    table = table_ref[...]
    table_rows = table.shape[0]
    turned_once = pltpu.roll(table, 127, 1)
    last = lax.broadcasted_iota(jnp.int32, table.shape, 1) == 127
    rise_table = jnp.where(last, pltpu.roll(turned_once, table_rows - 1, 0), turned_once) - table
    base = jnp.zeros((own, stn), F32)
    rise = jnp.zeros((own, stn), F32)
    for row in range(table_rows):
        here = upper == row
        b_row = jnp.broadcast_to(table[row:row + 1], (own, 128))
        s_row = jnp.broadcast_to(rise_table[row:row + 1], (own, 128))
        b_new, s_new = [], []
        for part in range(parts):
            at = lower[:, part * 128:(part + 1) * 128]
            b_new.append(jnp.take_along_axis(b_row, at, axis=1, mode="promise_in_bounds"))
            s_new.append(jnp.take_along_axis(s_row, at, axis=1, mode="promise_in_bounds"))
        base = jnp.where(here, jnp.concatenate(b_new, 1), base)
        rise = jnp.where(here, jnp.concatenate(s_new, 1), rise)
    delays = base + fraction.astype(F32) * (1.0 / 65536.0) * rise
    angle = delays * (-2.0 * math.pi / NFFT)
    turn_re, turn_im = jnp.cos(angle), jnp.sin(angle)
    masks = [jnp.where(group == g, math.sqrt(GROUPS / STATIONS), 0.0) for g in range(GROUPS)]

    lane = lax.broadcasted_iota(jnp.int32, (OUT, KB, TAPS * KB), 2) % KB
    sample = lax.broadcasted_iota(jnp.int32, (OUT, KB, TAPS * KB), 1)
    diagonal = lane == sample
    blocks = NFFT // KB

    def filter_block(kb, _):
        slot = kb % 2
        fetch(kb, slot).wait()

        @pl.when(kb + 1 < blocks)
        def _():
            fetch(kb + 1, 1 - slot).start()

        taps = rows_ref[kb]
        taps = jnp.where(core == 0, taps, pltpu.roll(taps, TAPS, 0))
        lhs = jnp.where(diagonal, taps[:, None, :], 0.0).reshape(OUT * KB, TAPS * KB).astype(BF16)
        at = pl.ds(pl.multiple_of(kb * KB, KB), KB)
        for p in range(POL):
            for i in range(2):
                rhs = vbuf[slot, p, :, i].reshape(TAPS * KB, stn)
                made = jnp.dot(lhs, rhs, preferred_element_type=F32)
                filt[p * OUT:(p + 1) * OUT, i, at, :] = made.reshape(OUT, KB, stn).astype(BF16)
        return 0

    lax.fori_loop(0, blocks, filter_block, 0)

    first = lax.broadcasted_iota(jnp.int32, (half, stn), 0) == 0

    def transform(frame, _):
        r = jnp.dot(dft_ref[...], filt[frame, 0], preferred_element_type=F32)
        i = jnp.dot(dft_ref[...], filt[frame, 1], preferred_element_type=F32)
        c_re, s_re, c_im, s_im = r[:half], r[half:], i[:half], i[half:]
        at = pl.ds(pl.multiple_of(frame * 8, 8), 8)
        values = (
            jnp.where(first, c_re, c_re + s_im),
            jnp.where(first, c_im, c_im - s_re),
            jnp.where(first, s_re, c_re - s_im),
            jnp.where(first, s_im, c_im + s_re),
        )
        for which, value in enumerate(values):
            for part in range(parts):
                spec[which, part, :, at, :] = value[:, part * 128:(part + 1) * 128].reshape(half // 8, 8, 128)
        return 0

    lax.fori_loop(0, POL * OUT, transform, 0, unroll=UNROLL_T)

    rows = POL * OUT
    lanes = lax.broadcasted_iota(jnp.int32, (rows, 128), 1)
    minus_low = jnp.where(lanes < 64, -1.0, 1.0)
    minus_high = -minus_low
    even_chunk = lanes[:OUT] // 32 % 2 == 0
    top = lax.broadcasted_iota(jnp.int32, (OUT, 128), 0) < TAPS

    def take(which, c):
        tile, line = c // 8 % (half // 8), c % 8
        found = [spec[which, part, tile, pl.ds(line, rows, stride=8), :] for part in range(parts)]
        return jnp.concatenate(found, axis=1).astype(BF16)

    def weights(w_re, w_im):
        made = []
        for value in (w_re, w_im):
            for h in range(2):
                for g in range(GROUPS):
                    made.append(value[h * own // 2:(h + 1) * own // 2] * masks[g])
        return jnp.concatenate(made, axis=0).astype(BF16)

    def times(lhs, w):
        return lax.dot_general(lhs, w, (((1,), (1,)), ((), ())), preferred_element_type=F32)

    def positive(re, im):
        return re + minus_low * pltpu.roll(im, 64, 1)

    def negative(re, im):
        return minus_high * re + pltpu.roll(im, 64, 1)

    def both(c, w):
        made = times(jnp.concatenate([take(which, c) for which in range(4)], axis=0), weights(*w))
        return positive(made[:rows], made[rows:2 * rows]), negative(made[2 * rows:3 * rows], made[3 * rows:])

    def by_half(value):
        a, b = value[:OUT], value[OUT:]
        return jnp.where(even_chunk, a, pltpu.roll(b, 32, 1)), jnp.where(even_chunk, pltpu.roll(a, 96, 1), b)

    def put(owner, q, slot, even, odd):
        at = owner % 4
        to_xl, to_core = at // 2, at % 2
        for h, (e, o) in enumerate(zip(by_half(even), by_half(odd))):
            pa[to_core, q, h, to_xl, slot, 0] = jnp.where(top, e, pltpu.roll(o, TAPS, 0)).astype(BF16)
            pa[to_core, q, h, to_xl, slot, 1] = jnp.where(top, pltpu.roll(e, TAPS, 0), o).astype(BF16)

    def turned(w):
        return (w[0] * turn_re - w[1] * turn_im, w[0] * turn_im + w[1] * turn_re)

    def chunk(t):
        return (t + z) % CHUNKS

    def make(t):
        q = chunk(t)
        begin = q * steps
        here = angle * (2 * begin).astype(F32)
        w = (jnp.cos(here), jnp.sin(here))
        made = times(jnp.concatenate([take(which, 2 * begin) for which in range(2)], axis=0), weights(*w))
        even = positive(made[:rows], made[rows:])
        w = turned(w)

        def pair(i, state):
            w_re, w_im, even = state
            e = begin + i
            odd, odd_minus = both(2 * e + 1, (w_re, w_im))
            w = turned((w_re, w_im))
            later, even_minus = both(2 * e + 2, w)
            w = turned(w)
            put(e, t, i // 4, even, odd)
            put(half - 1 - e, t, side + i // 4, even_minus, odd_minus)
            return w[0], w[1], later

        lax.fori_loop(0, steps, pair, (w[0], w[1], even), unroll=UNROLL_P)

    def place(t, slot):
        at = chunk(t) * side + slot % side
        return jnp.where(slot < side, at, count - 1 - at)

    lead = core == 0

    def pair_copy(t):
        return pltpu.make_async_remote_copy(
            src_ref=pa.at[1 - core, t], dst_ref=r0.at[t], send_sem=s0_sem.at[t], recv_sem=r0_sem.at[t],
            device_id=other, device_id_type=MESH)

    def row_copy(t, k):
        device, to = row_peer(k)
        return pltpu.make_async_remote_copy(
            src_ref=m.at[t, to // 2, to % 2], dst_ref=r1.at[t, xh * 2 + xl], send_sem=s1_sem.at[t, k - 1],
            recv_sem=r1_sem.at[t, k - 1], device_id=device, device_id_type=MESH)

    def own_copy(t):
        return pltpu.make_async_copy(m.at[t, xh, xl], r1.at[t, xh * 2 + xl], own_sem.at[t])

    def column_copy(t, slot, k):
        return pltpu.make_async_remote_copy(
            src_ref=s2.at[t, slot], dst_ref=out.at[zy], send_sem=s2_sem.at[k], recv_sem=r2_sem.at[k],
            device_id=column_peer(k), device_id_type=MESH)

    def merge(t):
        for h in range(2):
            for x in range(2):
                def body(i, _):
                    a0, a1 = pa[core, t, h, x, i, 0].astype(F32), pa[core, t, h, x, i, 1].astype(F32)
                    b0, b1 = r0[t, h, x, i, 0].astype(F32), r0[t, h, x, i, 1].astype(F32)
                    m[t, h, x, i, 0] = jnp.where(lead, a0, b0).astype(BF16)
                    m[t, h, x, i, 1] = (a1 + b1).astype(BF16)
                    m[t, h, x, i, 2] = jnp.where(lead, b0, a0).astype(BF16)
                    return 0
                lax.fori_loop(0, 2 * side, body, 0, unroll=True)

    def reduce(t):
        def body(i, _):
            s = [[r1[t, x, i, g].astype(F32) + r1[t, 2 + x, i, g].astype(F32) for g in range(3)] for x in range(2)]
            s2[t, i, 0] = s[0][0].astype(BF16)
            s2[t, i, 1] = s[0][1].astype(BF16)
            s2[t, i, 2] = (s[0][2] + s[1][0]).astype(BF16)
            s2[t, i, 3] = s[1][1].astype(BF16)
            s2[t, i, 4] = s[1][2].astype(BF16)
            return 0
        lax.fori_loop(0, 2 * side, body, 0, unroll=True)

    pl.semaphore_wait(barrier, 4 + count - 1)

    def run(t, _):
        @pl.when(t < CHUNKS)
        def _():
            make(t)
            pair_copy(t).start()

        @pl.when(jnp.logical_and(t >= 1, t <= CHUNKS))
        def _():
            pair_copy(t - 1).wait()
            merge(t - 1)
            for k in (2, 1, 3):
                row_copy(t - 1, k).start()
            own_copy(t - 1).start()

        @pl.when(t >= LAG)
        def _():
            for k in (2, 1, 3):
                row_copy(t - LAG, k).wait()
            own_copy(t - LAG).wait()
            reduce(t - LAG)

            def send(slot, _):
                k = (place(t - LAG, slot) + count - zy) % count

                @pl.when(k != 0)
                def _():
                    column_copy(t - LAG, slot, k).start()

                @pl.when(k == 0)
                def _():
                    mine = pltpu.make_async_copy(s2.at[t - LAG, slot], out.at[zy], mine_sem)
                    mine.start()
                    mine.wait()
                return 0

            lax.fori_loop(0, 2 * side, send, 0)

        return 0

    lax.fori_loop(0, CHUNKS + LAG, run, 0)

    def finish(k, _):
        column_copy(0, 0, k).wait()
        return 0

    lax.fori_loop(1, count, finish, 0)


def fused_call(v, rows, dft, table, index, fraction, group, nz, ny):
    stn = v.shape[-1]
    zy = nz * ny
    slots = zy // CHUNKS
    vmem = pl.BlockSpec(memory_space=pltpu.VMEM)
    dma = pltpu.SemaphoreType.DMA
    return pl.pallas_call(
        functools.partial(fused_kernel, nz, ny),
        out_shape=jax.ShapeDtypeStruct((zy, 5, OUT, 128), BF16),
        in_specs=[pl.BlockSpec(memory_space=pl.ANY)] + [vmem] * 6,
        out_specs=vmem,
        scratch_shapes=[
            pltpu.VMEM((2, POL, TAPS, 2, KB, stn), BF16),
            pltpu.VMEM((POL * OUT, 2, NFFT, stn), BF16),
            pltpu.VMEM((4, stn // 128, NFFT // 16, POL * OUT * 8, 128), F32),
            pltpu.VMEM((stn // 64, index.shape[0], 128), jnp.int32),
            pltpu.VMEM((2, CHUNKS, 2, 2, slots, 2, OUT, 128), BF16),
            pltpu.VMEM((CHUNKS, 2, 2, slots, 2, OUT, 128), BF16),
            pltpu.VMEM((CHUNKS, 2, 2, slots, 3, OUT, 128), BF16),
            pltpu.VMEM((CHUNKS, 4, slots, 3, OUT, 128), BF16),
            pltpu.VMEM((CHUNKS, slots, 5, OUT, 128), BF16),
            dma((2,)), dma((CHUNKS,)), dma((CHUNKS,)), dma((CHUNKS,)), dma((CHUNKS, 3)), dma((CHUNKS, 3)),
            dma((zy,)), dma((zy,)), dma,
        ],
        compiler_params=pltpu.CompilerParams(
            collective_id=0, has_side_effects=True, vmem_limit_bytes=62 * 1024 * 1024),
        name="beams",
    )(v, rows, dft, table, index, fraction, group)


def finish_kernel(x_ref, out_ref, frames):
    blocks = x_ref.shape[0]
    top = lax.broadcasted_iota(jnp.int32, (OUT, 128), 0) < TAPS
    span = 4 * TAPS

    def gather(b, _):
        segs = [x_ref[b, g].astype(F32) for g in range(4)]
        before = x_ref[jnp.maximum(b - 1, 0), 4].astype(F32)
        segs[0] = segs[0] + jnp.where(b > 0, before, 0.0)
        for j in range(2):
            a, c = segs[2 * j], segs[2 * j + 1]
            at = pl.ds(pl.multiple_of(b * span + j * OUT, 8), OUT)
            frames[0, at, :] = jnp.where(top, a, pltpu.roll(c, TAPS, 0))
            frames[1, at, :] = jnp.where(top, pltpu.roll(a, TAPS, 0), c)
        return 0

    lax.fori_loop(0, blocks, gather, 0)

    def turn(t, _):
        at = pl.ds(pl.multiple_of(t * 128, 128), 128)
        a, c = frames[0, at, :].T, frames[1, at, :].T
        both = jnp.stack([a, c], axis=1).astype(BF16)
        for ro in range(2):
            for p in range(POL):
                for g in range(GROUPS):
                    for jj in range(8):
                        out_ref[ro, 4 * jj + g, p, :, at] = both[ro * 64 + p * 32 + g * 8 + jj]
        return 0

    lax.fori_loop(0, blocks * span // 128, turn, 0)


def finish_call(x):
    blocks = x.shape[0]
    total = blocks * 4 * TAPS
    vmem = pl.BlockSpec(memory_space=pltpu.VMEM)
    return pl.pallas_call(
        finish_kernel,
        out_shape=jax.ShapeDtypeStruct((2, 32, POL, 2, total), BF16),
        in_specs=[vmem],
        out_specs=vmem,
        scratch_shapes=[pltpu.VMEM((2, total, 128), F32)],
        compiler_params=pltpu.CompilerParams(vmem_limit_bytes=32 * 1024 * 1024),
        name="finish",
    )(x)


def shards(voltages, delay_table, delay_index, delay_fraction, station_subarray):
    nz, ny = lax.axis_size("z"), lax.axis_size("y")
    rows = jnp.asarray(filter_rows())
    dft = jnp.asarray(dft_rows()).astype(BF16)
    found = fused_call(voltages, rows, dft, delay_table.reshape(-1, 128), delay_index, delay_fraction,
                       station_subarray.reshape(1, -1), nz, ny)
    return finish_call(found)


def solution(mesh):
    torus = Mesh(mesh.devices.reshape(8, 4, 2, 2, mesh.shape["stn"]), CHAN + ("stn",))
    placed = (P(None, CHAN, None, None, "stn"), P(), P(None, "stn"), P(None, "stn"), P("stn"))
    return jax.shard_map(
        shards,
        mesh=torus,
        in_specs=placed,
        out_specs=P(None, "stn", None, CHAN, None),
        check_vma=False,
    )
```

time: 135 us -> 89.4 us (0.66)
  Pallas kernels: 127 us -> 87.5 us
  local copies, waits for them, and re-layouts: 5.71 us -> 1.19 us
  other arithmetic: 2.04 us -> 0 us
    pallas_call x2 -> x1, Pallas kernels: 123 us -> 84 us  [fused_call(): pl.pallas_call(functools.partial(fused_kernel, nz, ny), out_shape=jax.Sha...]
    slice x2 -> x0, local copies, waits for them, and re-layouts: 2.06 us -> none  [shards(): step = jnp.concatenate([delay_table[1:], delay_table[-1:]]) - delay_table]
    reshape x1 -> x0, other arithmetic: 2.04 us -> none  [shards(): step.reshape(-1, 128)]
    squeeze x1 -> x0, local copies, waits for them, and re-layouts: 1.77 us -> none  [shards(): lax.dynamic_index_in_dim(jnp.asarray(filter_rows()), lax.axis_index('core...]
where the time goes in v2:
time: 89.4 us; the launch traced here: 88.7 us
  Pallas kernels  87.5 us (98%)
  local copies, waits for them, and re-layouts  1.19 us (1%)
    pallas_call x1, Pallas kernels, fused_call(): pl.pallas_call(functools.partial(fused_kernel, nz, ny), out_shape=jax.Sha...  84 us
    pallas_call x1, Pallas kernels, finish_call(): pl.pallas_call(finish_kernel, out_shape=jax.ShapeDtypeStruct((2, 32, POL,...  3.42 us

profile of v2, /device:TPU:24, one launch (start us, length us, event | category | flops | bytes accessed | tf_op | source)
XLA Modules:
  0.0 88.7 jit_solution(2608528738617781921)
XLA Ops:
  0.0 84.0 %beams.1.x_ref = bf16[32,5,24,128]{3,2,1,0:T(8,128)(2,1)} custom-call(bf16[2,12,2,256,256]{4,3,2,1,0:T(8,128)(2,1)} %v_hbm.1, f32[16,24,192]{2,1,0:T(8,128)} %constant.4.clone.rows_ref, bf16[256,256]{1,0:T(8,128)(2,1)} %constant.7.dft_ref, f32[32,128]{1,0:T(8,128)} %bitcast.2, s32[64,256]{1,0:T(8,128)} %index_ref.1, s32[64,256]{1,0:T(8,128)} %fraction_ref.1, ...), custom_call_target="tpu_custom_call" | custom-call | tf_op jit(solution)/shard_map/beams/pallas_call | solution.py:360
  84.0 0.0 copy-start
  84.1 1.2 %copy-done = bf16[32,5,24,128]{3,2,1,0:T(8,128)(2,1)S(1)} copy-done((bf16[32,5,24,128]{3,2,1,0:T(8,128)(2,1)S(1)}, bf16[32,5,24,128]{3,2,1,0:T(8,128)(2,1)}, u32[]{:S(2)}) %copy-start) | copy-done | bytes 983064
  85.2 3.4 %finish.1 = bf16[2,32,2,2,1536]{4,3,2,1,0:T(2,128)(2,1)} custom-call(bf16[32,5,24,128]{3,2,1,0:T(8,128)(2,1)S(1)} %copy-done), custom_call_target="tpu_custom_call" | custom-call | tf_op jit(solution)/shard_map/finish/pallas_call | solution.py:420
Async XLA Ops:
  84.0 1.2 %copy-start = (bf16[32,5,24,128]{3,2,1,0:T(8,128)(2,1)S(1)}, bf16[32,5,24,128]{3,2,1,0:T(8,128)(2,1)}, u32[]{:S(2)}) copy-start(bf16[32,5,24,128]{3,2,1,0:T(8,128)(2,1)} %beams.1.x_ref) | copy-start | bytes 2949124

commit v3 on v2

--- a/solution.py
+++ b/solution.py
@@ -20,10 +20,7 @@
 F32 = jnp.float32
 BF16 = jnp.bfloat16
 OUT = 2 * TAPS
-CHUNKS = 8
-LAG = 3
-UNROLL_T = 2
-UNROLL_P = 1
+LAG = 4
 KB = 16
 
 
@@ -69,16 +66,16 @@
     xl, core, xh = lax.axis_index("xl"), lax.axis_index("core"), lax.axis_index("stn")
     zy = z * ny + y
     count = nz * ny
-    steps = half // 2 // CHUNKS
-    side = count // CHUNKS // 2
+    chunks = count // 2
+    steps = half // 2 // chunks
 
     def row_peer(k):
-        place = (xh * 2 + xl + k) % 4
-        return (z, y, place % 2, core, place // 2), place
+        place = lax.rem(xh * 2 + xl + k, 4)
+        return (z, y, lax.rem(place, 2), core, lax.div(place, 2)), place
 
     def column_peer(k):
-        place = (zy + k) % count
-        return (place // ny, place % ny, xl, core, xh)
+        place = lax.rem(zy + k, count)
+        return (lax.div(place, ny), lax.rem(place, ny), xl, core, xh)
 
     other = (z, y, xl, 1 - core, xh)
     barrier = pltpu.get_barrier_semaphore()
@@ -111,7 +108,7 @@
     for g in range(GROUPS):
         index = jnp.where(group == g, every_fourth(0, g), index)
         fraction = jnp.where(group == g, every_fourth(parts, g), fraction)
-    upper, lower = index // 128, index % 128
+    upper, lower = lax.div(index, 128), lax.rem(index, 128)
     table = table_ref[...]
     table_rows = table.shape[0]
     turned_once = pltpu.roll(table, 127, 1)
@@ -141,7 +138,7 @@
     blocks = NFFT // KB
 
     def filter_block(kb, _):
-        slot = kb % 2
+        slot = lax.rem(kb, 2)
         fetch(kb, slot).wait()
 
         @pl.when(kb + 1 < blocks)
@@ -159,7 +156,7 @@
                 filt[p * OUT:(p + 1) * OUT, i, at, :] = made.reshape(OUT, KB, stn).astype(BF16)
         return 0
 
-    lax.fori_loop(0, blocks, filter_block, 0)
+    lax.fori_loop(0, blocks, filter_block, 0, unroll=2)
 
     first = lax.broadcasted_iota(jnp.int32, (half, stn), 0) == 0
 
@@ -179,7 +176,7 @@
                 spec[which, part, :, at, :] = value[:, part * 128:(part + 1) * 128].reshape(half // 8, 8, 128)
         return 0
 
-    lax.fori_loop(0, POL * OUT, transform, 0, unroll=UNROLL_T)
+    lax.fori_loop(0, POL * OUT, transform, 0, unroll=2)
 
     rows = POL * OUT
     lanes = lax.broadcasted_iota(jnp.int32, (rows, 128), 1)
@@ -189,7 +186,7 @@
     top = lax.broadcasted_iota(jnp.int32, (OUT, 128), 0) < TAPS
 
     def take(which, c):
-        tile, line = c // 8 % (half // 8), c % 8
+        tile, line = lax.rem(lax.div(c, 8), half // 8), lax.rem(c, 8)
         found = [spec[which, part, tile, pl.ds(line, rows, stride=8), :] for part in range(parts)]
         return jnp.concatenate(found, axis=1).astype(BF16)
 
@@ -210,52 +207,44 @@
     def negative(re, im):
         return minus_high * re + pltpu.roll(im, 64, 1)
 
-    def both(c, w):
-        made = times(jnp.concatenate([take(which, c) for which in range(4)], axis=0), weights(*w))
-        return positive(made[:rows], made[rows:2 * rows]), negative(made[2 * rows:3 * rows], made[3 * rows:])
+    def beamed(c, w, signs):
+        made = times(jnp.concatenate([take(2 * sign + i, c) for sign in signs for i in range(2)], axis=0), weights(*w))
+        found = []
+        for n, sign in enumerate(signs):
+            re, im = made[2 * n * rows:(2 * n + 1) * rows], made[(2 * n + 1) * rows:(2 * n + 2) * rows]
+            found.append(negative(re, im) if sign else positive(re, im))
+        return found
 
     def by_half(value):
         a, b = value[:OUT], value[OUT:]
         return jnp.where(even_chunk, a, pltpu.roll(b, 32, 1)), jnp.where(even_chunk, pltpu.roll(a, 96, 1), b)
 
-    def put(owner, q, slot, even, odd):
-        at = owner % 4
-        to_xl, to_core = at // 2, at % 2
+    def put(t, at, slot, even, odd):
         for h, (e, o) in enumerate(zip(by_half(even), by_half(odd))):
-            pa[to_core, q, h, to_xl, slot, 0] = jnp.where(top, e, pltpu.roll(o, TAPS, 0)).astype(BF16)
-            pa[to_core, q, h, to_xl, slot, 1] = jnp.where(top, pltpu.roll(e, TAPS, 0), o).astype(BF16)
+            pa[at % 2, t, h, at // 2, slot, 0] = jnp.where(top, e, pltpu.roll(o, TAPS, 0)).astype(BF16)
+            pa[at % 2, t, h, at // 2, slot, 1] = jnp.where(top, pltpu.roll(e, TAPS, 0), o).astype(BF16)
 
     def turned(w):
         return (w[0] * turn_re - w[1] * turn_im, w[0] * turn_im + w[1] * turn_re)
 
     def chunk(t):
-        return (t + z) % CHUNKS
+        return lax.rem(t + z, chunks // ny) * ny + lax.rem(lax.div(t, chunks // ny) + y, ny)
 
     def make(t):
-        q = chunk(t)
-        begin = q * steps
-        here = angle * (2 * begin).astype(F32)
+        begin = chunk(t) * (2 * steps)
+        here = angle * begin.astype(F32)
         w = (jnp.cos(here), jnp.sin(here))
-        made = times(jnp.concatenate([take(which, 2 * begin) for which in range(2)], axis=0), weights(*w))
-        even = positive(made[:rows], made[rows:])
-        w = turned(w)
-
-        def pair(i, state):
-            w_re, w_im, even = state
-            e = begin + i
-            odd, odd_minus = both(2 * e + 1, (w_re, w_im))
-            w = turned((w_re, w_im))
-            later, even_minus = both(2 * e + 2, w)
+        even, = beamed(begin, w, (0,))
+        for e in range(steps):
             w = turned(w)
-            put(e, t, i // 4, even, odd)
-            put(half - 1 - e, t, side + i // 4, even_minus, odd_minus)
-            return w[0], w[1], later
-
-        lax.fori_loop(0, steps, pair, (w[0], w[1], even), unroll=UNROLL_P)
-
-    def place(t, slot):
-        at = chunk(t) * side + slot % side
-        return jnp.where(slot < side, at, count - 1 - at)
+            odd, odd_minus = beamed(begin + 2 * e + 1, w, (0, 1))
+            put(t, e, 0, even, odd)
+            w = turned(w)
+            if e < steps - 1:
+                even, even_minus = beamed(begin + 2 * e + 2, w, (0, 1))
+            else:
+                even_minus, = beamed(begin + 2 * e + 2, w, (1,))
+            put(t, steps - 1 - e, 1, even_minus, odd_minus)
 
     lead = core == 0
 
@@ -288,7 +277,7 @@
                     m[t, h, x, i, 1] = (a1 + b1).astype(BF16)
                     m[t, h, x, i, 2] = jnp.where(lead, b0, a0).astype(BF16)
                     return 0
-                lax.fori_loop(0, 2 * side, body, 0, unroll=True)
+                lax.fori_loop(0, 2, body, 0, unroll=True)
 
     def reduce(t):
         def body(i, _):
@@ -299,17 +288,17 @@
             s2[t, i, 3] = s[1][1].astype(BF16)
             s2[t, i, 4] = s[1][2].astype(BF16)
             return 0
-        lax.fori_loop(0, 2 * side, body, 0, unroll=True)
+        lax.fori_loop(0, 2, body, 0, unroll=True)
 
     pl.semaphore_wait(barrier, 4 + count - 1)
 
     def run(t, _):
-        @pl.when(t < CHUNKS)
+        @pl.when(t < chunks)
         def _():
             make(t)
             pair_copy(t).start()
 
-        @pl.when(jnp.logical_and(t >= 1, t <= CHUNKS))
+        @pl.when(jnp.logical_and(t >= 1, t <= chunks))
         def _():
             pair_copy(t - 1).wait()
             merge(t - 1)
@@ -324,25 +313,23 @@
             own_copy(t - LAG).wait()
             reduce(t - LAG)
 
-            def send(slot, _):
-                k = (place(t - LAG, slot) + count - zy) % count
+            for slot in range(2):
+                to = chunk(t - LAG)
+                k = lax.rem((count - 1 - to if slot else to) + count - zy, count)
 
                 @pl.when(k != 0)
-                def _():
+                def _(slot=slot, k=k):
                     column_copy(t - LAG, slot, k).start()
 
                 @pl.when(k == 0)
-                def _():
+                def _(slot=slot):
                     mine = pltpu.make_async_copy(s2.at[t - LAG, slot], out.at[zy], mine_sem)
                     mine.start()
                     mine.wait()
-                return 0
-
-            lax.fori_loop(0, 2 * side, send, 0)
-
-        return 0
-
-    lax.fori_loop(0, CHUNKS + LAG, run, 0)
+
+        return 0
+
+    lax.fori_loop(0, chunks + LAG, run, 0)
 
     def finish(k, _):
         column_copy(0, 0, k).wait()
@@ -354,7 +341,8 @@
 def fused_call(v, rows, dft, table, index, fraction, group, nz, ny):
     stn = v.shape[-1]
     zy = nz * ny
-    slots = zy // CHUNKS
+    chunks = zy // 2
+    slots = 2
     vmem = pl.BlockSpec(memory_space=pltpu.VMEM)
     dma = pltpu.SemaphoreType.DMA
     return pl.pallas_call(
@@ -367,12 +355,12 @@
             pltpu.VMEM((POL * OUT, 2, NFFT, stn), BF16),
             pltpu.VMEM((4, stn // 128, NFFT // 16, POL * OUT * 8, 128), F32),
             pltpu.VMEM((stn // 64, index.shape[0], 128), jnp.int32),
-            pltpu.VMEM((2, CHUNKS, 2, 2, slots, 2, OUT, 128), BF16),
-            pltpu.VMEM((CHUNKS, 2, 2, slots, 2, OUT, 128), BF16),
-            pltpu.VMEM((CHUNKS, 2, 2, slots, 3, OUT, 128), BF16),
-            pltpu.VMEM((CHUNKS, 4, slots, 3, OUT, 128), BF16),
-            pltpu.VMEM((CHUNKS, slots, 5, OUT, 128), BF16),
-            dma((2,)), dma((CHUNKS,)), dma((CHUNKS,)), dma((CHUNKS,)), dma((CHUNKS, 3)), dma((CHUNKS, 3)),
+            pltpu.VMEM((2, chunks, 2, 2, slots, 2, OUT, 128), BF16),
+            pltpu.VMEM((chunks, 2, 2, slots, 2, OUT, 128), BF16),
+            pltpu.VMEM((chunks, 2, 2, slots, 3, OUT, 128), BF16),
+            pltpu.VMEM((chunks, 4, slots, 3, OUT, 128), BF16),
+            pltpu.VMEM((chunks, slots, 5, OUT, 128), BF16),
+            dma((2,)), dma((chunks,)), dma((chunks,)), dma((chunks,)), dma((chunks, 3)), dma((chunks, 3)),
             dma((zy,)), dma((zy,)), dma,
         ],
         compiler_params=pltpu.CompilerParams(

time: 89.4 us -> 76 us (0.85)
  the two profiles are of different devices: /device:TPU:24 before, /device:TPU:40 now
where the time goes in v3:
time: 76 us; the launch traced here: 75.2 us
  Pallas kernels  74 us (97%)
  local copies, waits for them, and re-layouts  1.19 us (2%)
    pallas_call x1, Pallas kernels, fused_call(): pl.pallas_call(functools.partial(fused_kernel, nz, ny), out_shape=jax.Sha...  70.6 us
    pallas_call x1, Pallas kernels, finish_call(): pl.pallas_call(finish_kernel, out_shape=jax.ShapeDtypeStruct((2, 32, POL,...  3.42 us

profile of v3, /device:TPU:40, one launch (start us, length us, event | category | flops | bytes accessed | tf_op | source)
XLA Modules:
  0.0 75.2 jit_solution(17947751696695061719)
XLA Ops:
  0.0 70.6 %beams.1.x_ref = bf16[32,5,24,128]{3,2,1,0:T(8,128)(2,1)} custom-call(bf16[2,12,2,256,256]{4,3,2,1,0:T(8,128)(2,1)} %v_hbm.1, f32[16,24,192]{2,1,0:T(8,128)} %constant.4.clone.rows_ref, bf16[256,256]{1,0:T(8,128)(2,1)} %constant.7.dft_ref, f32[32,128]{1,0:T(8,128)} %bitcast.2, s32[64,256]{1,0:T(8,128)} %index_ref.1, s32[64,256]{1,0:T(8,128)} %fraction_ref.1, ...), custom_call_target="tpu_custom_call" | custom-call | tf_op jit(solution)/shard_map/beams/pallas_call | solution.py:348
  70.6 0.0 copy-start
  70.6 1.2 %copy-done = bf16[32,5,24,128]{3,2,1,0:T(8,128)(2,1)S(1)} copy-done((bf16[32,5,24,128]{3,2,1,0:T(8,128)(2,1)S(1)}, bf16[32,5,24,128]{3,2,1,0:T(8,128)(2,1)}, u32[]{:S(2)}) %copy-start) | copy-done | bytes 983064
  71.8 3.4 %finish.1 = bf16[2,32,2,2,1536]{4,3,2,1,0:T(2,128)(2,1)} custom-call(bf16[32,5,24,128]{3,2,1,0:T(8,128)(2,1)S(1)} %copy-done), custom_call_target="tpu_custom_call" | custom-call | tf_op jit(solution)/shard_map/finish/pallas_call | solution.py:408
Async XLA Ops:
  70.6 1.2 %copy-start = (bf16[32,5,24,128]{3,2,1,0:T(8,128)(2,1)S(1)}, bf16[32,5,24,128]{3,2,1,0:T(8,128)(2,1)}, u32[]{:S(2)}) copy-start(bf16[32,5,24,128]{3,2,1,0:T(8,128)(2,1)} %beams.1.x_ref) | copy-start | bytes 2949124
